TPU v7x, 32 devices: a whole 2x2x4 slice. The times are simulated.
32 devices in a mesh: seq: 8 (over z, y), head: 4 (over x, core).
Axes of the slice: x: 2, y: 2, z: 4, core: 2. Of those that a mesh axis runs over, the one named last changes fastest.
Arguments:
- query: bfloat16 [4096, 8192], P('seq', 'head'), may hold values from -1.5 to 1.5
- key_in: bfloat16 [4096, 8192], P('seq', 'head'), may hold values from -0.5 to 0.5
- value: bfloat16 [4096, 8192], P('seq', 'head'), may hold values from -6 to 6
- gate: bfloat16 [4096, 8192], P(('seq', 'head')), may hold values from -6 to 6
- gain: float32 [8192], replicated, may hold values from 0.5 to 1.5
- grad_out: bfloat16 [4096, 8192], P(('seq', 'head')), may hold values from -6 to 6
Outputs:
- grad_query: bfloat16 [4096, 8192], P('seq', 'head')
- grad_key: bfloat16 [4096, 8192], P('seq', 'head')
- grad_value: bfloat16 [4096, 8192], P('seq', 'head')
- grad_gate: bfloat16 [4096, 8192], P(('seq', 'head'))
All inputs are finite; a program needn't handle non-finite values.
Results may differ from a plain program's by a relative error of at most 0.012.
Values may be sent and summed in bfloat16 or wider, within the bound.
A program may use at most 128 MiB of HBM per device.

v0:
```python
import functools

import jax
import jax.numpy as jnp
from jax import lax
from jax.experimental import pallas as pl
from jax.experimental.pallas import tpu as pltpu
from jax.sharding import PartitionSpec as P

HEAD_DIM = 128
EPS = 1e-06
MESH = pl.DeviceIdType.MESH
F32 = jnp.float32
BF16 = jnp.bfloat16
FORWARD_LAG = 3
BACKWARD_LAG = 3


def dot_nn(a, b):
    return lax.dot_general(a, b, (((1,), (0,)), ((), ())), preferred_element_type=F32)


def dot_nt(a, b):
    return lax.dot_general(a, b, (((1,), (1,)), ((), ())), preferred_element_type=F32)


def dot_tn(a, b):
    return lax.dot_general(a, b, (((0,), (0,)), ((), ())), preferred_element_type=F32)


def body(
    n_seq, n_head,
    q_h, k_h, v_h, gate_h, gain_h, go_h,
    gqv, gkv, gvv, ggv,
    q, k, v, gate, gain, go,
    wsend, wbuf, g2, attn, d_o, arows,
    st, st_p, st_c, st_o, pre,
    gst, gst_p, gst_c, gst_o,
    suf, scores, acc_a, acc_b,
    zbuf, stat_s, stat_r, inv_b, c_b,
    in_sem,
    w_ss, w_rs, a_ss, a_rs, s_ss, s_rs,
    p_ss, p_rs, c_ss, c_rs, gp_ss, gp_rs, gc_ss, gc_rs,
):
    hd = HEAD_DIM
    tok, cols = q.shape
    rows, width = gate.shape
    heads = cols // hd
    half = tok // 2
    idx = lax.axis_index("seq")
    me = lax.axis_index("head")
    side = lax.rem(idx, 2)
    partner = idx + 1 - 2 * side
    has_below = idx >= 2
    has_above = idx + 2 < n_seq
    order = [n_head // 2] + [d for d in range(1, n_head) if d != n_head // 2]

    def to_peer(d):
        return lax.rem(me + d, n_head)

    def from_peer(d):
        return lax.rem(me + n_head - d, n_head)

    loads = [
        pltpu.make_async_copy(src, dst, in_sem.at[i])
        for i, (src, dst) in enumerate(
            ((k_h, k), (v_h, v), (gain_h, gain), (gate_h, gate), (go_h, go), (q_h, q))
        )
    ]
    for load in loads:
        load.start()

    barrier = pltpu.get_barrier_semaphore()
    for d in range(1, n_head):
        pl.semaphore_signal(barrier, inc=1, device_id={"head": to_peer(d)}, device_id_type=MESH)
    pl.semaphore_signal(barrier, inc=1, device_id={"seq": partner}, device_id_type=MESH)

    @pl.when(has_below)
    def _():
        pl.semaphore_signal(barrier, inc=1, device_id={"seq": idx - 2}, device_id_type=MESH)

    @pl.when(has_above)
    def _():
        pl.semaphore_signal(barrier, inc=1, device_id={"seq": idx + 2}, device_id_type=MESH)

    below, above = has_below.astype(jnp.int32), has_above.astype(jnp.int32)
    pl.semaphore_wait(barrier, n_head + below + above)

    def head_cols(h):
        return pl.ds(pl.multiple_of(h * hd, hd), hd)

    br, bc = 32, 512
    n_bc = cols // bc
    n_blocks = (rows // br) * n_bc

    def block_at(i, start):
        r = pl.multiple_of((i // n_bc) * br, br)
        c = lax.rem(i, n_bc) * bc
        return r, pl.multiple_of(c, bc), pl.multiple_of(start + c, bc)

    def weigh(shard, local):
        start = shard * cols

        def step(i, carry):
            r, c, at = block_at(i, start)
            g = gate[pl.ds(r, br), pl.ds(at, bc)].astype(F32)
            scaled = go[pl.ds(r, br), pl.ds(at, bc)].astype(F32) * gain[:, pl.ds(at, bc)]
            sig = jax.nn.sigmoid(g)
            part = scaled * sig
            g2[pl.ds(r, br), pl.ds(at, bc)] = part * (1.0 + g * (1.0 - sig))
            weighted = (part * g).astype(BF16)
            if local:
                wbuf[pl.ds(pl.multiple_of(me * rows + r, br), br), pl.ds(c, bc)] = weighted
            else:
                wsend[pl.ds(r, br), pl.ds(at, bc)] = weighted
            return carry

        lax.fori_loop(0, n_blocks, step, 0)

    def row_block(shard):
        return pl.ds(pl.multiple_of(shard * rows, rows), rows)

    def col_block(shard):
        return pl.ds(pl.multiple_of(shard * cols, cols), cols)

    def w_copy(d):
        return pltpu.make_async_remote_copy(
            src_ref=wsend.at[:, col_block(to_peer(d))],
            dst_ref=wbuf.at[row_block(me), :],
            send_sem=w_ss.at[d], recv_sem=w_rs.at[d],
            device_id={"head": to_peer(d)}, device_id_type=MESH,
        )

    def w_arrival(d):
        return pltpu.make_async_remote_copy(
            src_ref=wsend.at[:, col_block(to_peer(d))],
            dst_ref=wbuf.at[row_block(from_peer(d)), :],
            send_sem=w_ss.at[d], recv_sem=w_rs.at[d],
            device_id={"head": to_peer(d)}, device_id_type=MESH,
        )

    def a_copy(d):
        return pltpu.make_async_remote_copy(
            src_ref=attn.at[row_block(to_peer(d)), :],
            dst_ref=arows.at[:, col_block(me)],
            send_sem=a_ss.at[d], recv_sem=a_rs.at[d],
            device_id={"head": to_peer(d)}, device_id_type=MESH,
        )

    def a_arrival(d):
        return pltpu.make_async_remote_copy(
            src_ref=attn.at[row_block(to_peer(d)), :],
            dst_ref=arows.at[:, col_block(from_peer(d))],
            send_sem=a_ss.at[d], recv_sem=a_rs.at[d],
            device_id={"head": to_peer(d)}, device_id_type=MESH,
        )

    def s_copy(d):
        return pltpu.make_async_remote_copy(
            src_ref=stat_s, dst_ref=stat_r.at[d],
            send_sem=s_ss.at[d], recv_sem=s_rs.at[d],
            device_id={"head": to_peer(d)}, device_id_type=MESH,
        )

    def state_copy(src, dst, ss, rs, h, target):
        return pltpu.make_async_remote_copy(
            src_ref=src.at[h], dst_ref=dst.at[h],
            send_sem=ss.at[h], recv_sem=rs.at[h],
            device_id={"seq": target}, device_id_type=MESH,
        )

    for load in loads[:2]:
        load.wait()

    def send_state(h, carry):
        sl = head_cols(h)
        st[h] = dot_tn(k[:, sl], v[:, sl]).astype(BF16)
        state_copy(st, st_p, p_ss, p_rs, h, partner).start()
        return carry

    lax.fori_loop(0, heads, send_state, 0)

    for load in loads[2:5]:
        load.wait()
    for d in order:
        weigh(to_peer(d), False)
        w_copy(d).start()
    weigh(me, True)
    loads[5].wait()

    def pass_on(h, own, mate, chain, out, sems, source_ok, target_ok, target, wants_mate):
        mate_ss, mate_rs, chain_ss, chain_rs = sems
        state_copy(own, mate, mate_ss, mate_rs, h, partner).wait_recv()
        got = mate[h].astype(F32)

        @pl.when(source_ok)
        def _():
            state_copy(out, chain, chain_ss, chain_rs, h, target).wait_recv()

        @pl.when(jnp.logical_not(source_ok))
        def _():
            chain[h] = jnp.zeros((hd, hd), BF16)

        before = chain[h].astype(F32)

        @pl.when(target_ok)
        def _():
            out[h] = (before + got + own[h].astype(F32)).astype(BF16)
            state_copy(out, chain, chain_ss, chain_rs, h, target).start()

        return (before + wants_mate.astype(F32) * got).astype(BF16)

    at_row = lax.broadcasted_iota(jnp.int32, (half, half), 0)
    at_col = lax.broadcasted_iota(jnp.int32, (half, half), 1)

    def lower(x):
        return jnp.where(at_row >= at_col, x, 0.0).astype(BF16)

    def upper(x):
        return jnp.where(at_row <= at_col, x, 0.0).astype(BF16)

    depth = idx // 2
    pairs = n_seq // 2

    def forward_local(h):
        sl = head_cols(h)
        q0, q1 = q[:half, sl], q[half:, sl]
        k0, k1 = k[:half, sl], k[half:, sl]
        v0, v1 = v[:half, sl], v[half:, sl]
        acc_a[:half, sl] = dot_nn(lower(dot_nt(q0, k0)), v0)
        acc_a[half:, sl] = dot_nn(dot_nt(q1, k0).astype(BF16), v0) + dot_nn(
            lower(dot_nt(q1, k1)), v1
        )
        scores[h, 0] = upper(dot_nt(k0, q0))
        scores[h, 1] = dot_nt(k0, q1).astype(BF16)
        scores[h, 2] = upper(dot_nt(k1, q1))

    def forward(i, carry):
        @pl.when(i < heads)
        def _():
            forward_local(i)

        h = i - FORWARD_LAG * depth

        @pl.when((h >= 0) & (h < heads))
        def _():
            sl = head_cols(h)
            before = pass_on(
                h, st, st_p, st_c, st_o, (p_ss, p_rs, c_ss, c_rs),
                has_below, has_above, idx + 2, side,
            )
            pre[h] = before
            attn[:, sl] = (acc_a[:, sl] + dot_nn(q[:, sl], before)).astype(BF16)

        return carry

    lax.fori_loop(0, heads + FORWARD_LAG * (pairs - 1), forward, 0)

    for d in order:
        w_arrival(d).wait_recv()

    lane = lax.broadcasted_iota(jnp.int32, (64, hd), 1)

    def sums(i, carry):
        rs = pl.ds(pl.multiple_of(i * 64, 64), 64)
        squares = jnp.zeros((64, hd), F32)
        crossed = jnp.zeros((64, hd), F32)
        for h in range(heads):
            a = attn[rs, h * hd:(h + 1) * hd].astype(F32)
            w = wbuf[rs, h * hd:(h + 1) * hd].astype(F32)
            squares = squares + a * a
            crossed = crossed + a * w
        s0 = jnp.sum(squares, axis=1, keepdims=True)
        s1 = jnp.sum(crossed, axis=1, keepdims=True)
        zbuf[rs, :] = jnp.where(lane == 0, s0, jnp.where(lane == 1, s1, 0.0))
        return carry

    lax.fori_loop(0, tok // 64, sums, 0)
    stat_s[...] = jnp.transpose(zbuf[...])[:8]
    for d in order:
        s_copy(d).start()
    for d in order:
        a_copy(d).start()
    total = stat_s[...]
    for d in order:
        s_copy(d).wait_recv()
        total = total + stat_r[d]
    spread = jnp.transpose(jnp.concatenate([total, jnp.zeros((hd - 8, tok), F32)], axis=0))
    inv = lax.rsqrt(spread[:, 0:1] / width + EPS)
    inv_b[...] = jnp.broadcast_to(inv, (tok, hd))
    c_b[...] = jnp.broadcast_to(inv * inv * (spread[:, 1:2] / width), (tok, hd))

    def send_grad(h, carry):
        sl = head_cols(h)
        a = attn[:, sl].astype(F32)
        grad = (inv_b[...] * (wbuf[:, sl].astype(F32) - a * c_b[...])).astype(BF16)
        d_o[:, sl] = grad
        gst[h] = dot_tn(q[:, sl], grad).astype(BF16)
        state_copy(gst, gst_p, gp_ss, gp_rs, h, partner).start()
        return carry

    lax.fori_loop(0, heads, send_grad, 0)

    def backward_local(h):
        sl = head_cols(h)
        q0, q1 = q[:half, sl], q[half:, sl]
        k0, k1 = k[:half, sl], k[half:, sl]
        v0, v1 = v[:half, sl], v[half:, sl]
        d0, d1 = d_o[:half, sl], d_o[half:, sl]
        before = pre[h]
        gqv[:half, sl] = (dot_nn(lower(dot_nt(d0, v0)), k0) + dot_nt(d0, before)).astype(BF16)
        gqv[half:, sl] = (
            dot_nn(dot_nt(d1, v0).astype(BF16), k0)
            + dot_nn(lower(dot_nt(d1, v1)), k1)
            + dot_nt(d1, before)
        ).astype(BF16)
        acc_a[:half, sl] = dot_nn(upper(dot_nt(v0, d0)), q0) + dot_nn(
            dot_nt(v0, d1).astype(BF16), q1
        )
        acc_a[half:, sl] = dot_nn(upper(dot_nt(v1, d1)), q1)
        acc_b[:half, sl] = dot_nn(scores[h, 0], d0) + dot_nn(scores[h, 1], d1)
        acc_b[half:, sl] = dot_nn(scores[h, 2], d1)

    def backward(i, carry):
        @pl.when(i < heads)
        def _():
            backward_local(i)

        for t in range(2):
            h = 2 * (i - BACKWARD_LAG * (pairs - 1 - depth)) + t

            @pl.when((h >= 0) & (h < heads))
            def _():
                suf[h] = pass_on(
                    h, gst, gst_p, gst_c, gst_o, (gp_ss, gp_rs, gc_ss, gc_rs),
                    has_above, has_below, idx - 2, 1 - side,
                )

        return carry

    steps = max(heads, BACKWARD_LAG * (pairs - 1) + (heads + 1) // 2)
    lax.fori_loop(0, steps, backward, 0)

    def add_later(h, carry):
        sl = head_cols(h)
        after = suf[h]
        gkv[:, sl] = (acc_a[:, sl] + dot_nt(v[:, sl], after)).astype(BF16)
        gvv[:, sl] = (acc_b[:, sl] + dot_nn(k[:, sl], after)).astype(BF16)
        return carry

    lax.fori_loop(0, heads, add_later, 0)

    def finish(shard, local):
        start = shard * cols

        def step(i, carry):
            r, c, at = block_at(i, start)
            mine = pl.multiple_of(me * rows + r, br)
            if local:
                a = attn[pl.ds(mine, br), pl.ds(c, bc)]
            else:
                a = arows[pl.ds(r, br), pl.ds(at, bc)]
            scale = inv_b[pl.ds(mine, br), :][:, 0:1]
            ggv[pl.ds(r, br), pl.ds(at, bc)] = (
                g2[pl.ds(r, br), pl.ds(at, bc)] * (a.astype(F32) * scale)
            ).astype(BF16)
            return carry

        lax.fori_loop(0, n_blocks, step, 0)

    finish(me, True)
    for d in order:
        a_arrival(d).wait_recv()
        finish(from_peer(d), False)

    for d in order:
        w_copy(d).wait_send()
        s_copy(d).wait_send()
        a_copy(d).wait_send()

    def drain(h, carry):
        state_copy(st, st_p, p_ss, p_rs, h, partner).wait_send()
        state_copy(gst, gst_p, gp_ss, gp_rs, h, partner).wait_send()

        @pl.when(has_above)
        def _():
            state_copy(st_o, st_c, c_ss, c_rs, h, idx + 2).wait_send()

        @pl.when(has_below)
        def _():
            state_copy(gst_o, gst_c, gc_ss, gc_rs, h, idx - 2).wait_send()

        return carry

    lax.fori_loop(0, heads, drain, 0)


def store(a, b, c, d, a_h, b_h, c_h, d_h, sem):
    copies = [
        pltpu.make_async_copy(src, dst, sem.at[i])
        for i, (src, dst) in enumerate(((a, a_h), (b, b_h), (c, c_h), (d, d_h)))
    ]
    for copy in copies:
        copy.start()
    for copy in copies:
        copy.wait()


def on_device(n_seq, n_head, query, key_in, value, gate, gain, grad_out):
    tok, cols = query.shape
    rows, width = gate.shape
    heads = cols // HEAD_DIM
    wide = pltpu.VMEM((tok, cols), BF16)
    thin = pltpu.VMEM((rows, width), BF16)
    state = pltpu.VMEM((heads, HEAD_DIM, HEAD_DIM), BF16)
    token = pltpu.VMEM((tok, HEAD_DIM), F32)
    by_peer = pltpu.SemaphoreType.DMA((n_head,))
    by_head = pltpu.SemaphoreType.DMA((heads,))
    anywhere = pl.BlockSpec(memory_space=pl.ANY)
    on_chip = pl.BlockSpec(memory_space=pltpu.VMEM)
    sum_of = pltpu.VMEM((tok, cols), F32)
    results = pl.pallas_call(
        functools.partial(body, n_seq, n_head),
        out_shape=[wide, wide, wide, thin],
        in_specs=[anywhere] * 6,
        out_specs=[on_chip] * 4,
        scratch_shapes=[
            wide, wide, wide, thin, pltpu.VMEM((1, width), F32), thin,
            thin, wide, pltpu.VMEM((rows, width), F32), wide, wide, thin,
            state, state, state, state, state,
            state, state, state, state,
            state, pltpu.VMEM((heads, 3, tok // 2, tok // 2), BF16), sum_of, sum_of,
            token, pltpu.VMEM((8, tok), F32), pltpu.VMEM((n_head, 8, tok), F32), token, token,
            pltpu.SemaphoreType.DMA((6,)),
            by_peer, by_peer, by_peer, by_peer, by_peer, by_peer,
            by_head, by_head, by_head, by_head, by_head, by_head, by_head, by_head,
        ],
        compiler_params=pltpu.CompilerParams(
            collective_id=0, has_side_effects=True, vmem_limit_bytes=52 * 2**20
        ),
        name="linear_attention_backward",
    )(query, key_in, value, gate, gain.reshape(1, width), grad_out)
    return pl.pallas_call(
        store,
        out_shape=[jax.ShapeDtypeStruct(x.shape, BF16) for x in results],
        in_specs=[on_chip] * 4,
        out_specs=[anywhere] * 4,
        scratch_shapes=[pltpu.SemaphoreType.DMA((4,))],
        compiler_params=pltpu.CompilerParams(vmem_limit_bytes=2**20),
        name="store_gradients",
    )(*[pltpu.with_memory_space_constraint(x, pltpu.VMEM) for x in results])


def solution(mesh):
    in_specs = (
        P("seq", "head"),
        P("seq", "head"),
        P("seq", "head"),
        P(("seq", "head"), None),
        P(),
        P(("seq", "head"), None),
    )
    out_specs = (P("seq", "head"), P("seq", "head"), P("seq", "head"), P(("seq", "head"), None))
    return jax.shard_map(
        functools.partial(on_device, mesh.shape["seq"], mesh.shape["head"]),
        mesh=mesh, in_specs=in_specs, out_specs=out_specs, check_vma=False,
    )
```

profile of v0, /device:TPU:0, one launch (start us, length us, event | category | flops | bytes accessed | tf_op | source)
XLA Modules:
  0.0 79.0 jit_solution(3104370361672134906)
XLA Ops:
  0.6 75.0 %linear_attention_backward.1 = (bf16[512,2048]{1,0:T(8,128)(2,1)S(1)}, bf16[512,2048]{1,0:T(8,128)(2,1)S(1)}, bf16[512,2048]{1,0:T(8,128)(2,1)S(1)}, bf16[128,8192]{1,0:T(8,128)(2,1)S(1)}) custom-call(bf16[512,2048]{1,0:T(8,128)(2,1)} %q_h.1, bf16[512,2048]{1,0:T(8,128)(2,1)} %k_h.1, bf16[512,2048]{1,0:T(8,128)(2,1)} %v_h.1, bf16[128,8192]{1,0:T(8,128)(2,1)} %gate_h.1, ...), custom_call_target="tpu_custom_call" | custom-call | tf_op jit(solution)/shard_map/linear_attention_backward/pallas_call | solution.py:422
  75.6 3.4 %store_gradients.1 = (bf16[512,2048]{1,0:T(8,128)(2,1)}, bf16[512,2048]{1,0:T(8,128)(2,1)}, bf16[512,2048]{1,0:T(8,128)(2,1)}, bf16[128,8192]{1,0:T(8,128)(2,1)}) custom-call(bf16[512,2048]{1,0:T(8,128)(2,1)S(1)} %get-tuple-element.8.a, bf16[512,2048]{1,0:T(8,128)(2,1)S(1)} %get-tuple-element.9.b, bf16[512,2048]{1,0:T(8,128)(2,1)S(1)} %get-tuple-element.10.c, ...), custom_call_target="tpu_custom_call" | custom-call | tf_op jit(solution)/shard_map/store_gradients/pallas_call | solution.py:443
where the time goes:
time: 79.2 us; the launch traced here: 79 us
  Pallas kernels  78.4 us (99%)
    pallas_call x1, Pallas kernels, on_device(): pl.pallas_call(functools.partial(body, n_seq, n_head), out_shape=[wide, w...  75 us
    pallas_call x1, Pallas kernels, on_device(): pl.pallas_call(store, out_shape=[jax.ShapeDtypeStruct(x.shape, BF16) for...  3.37 us

commit v1 on v0

v1 whole, which is shorter than its diff:
```python
import functools

import jax
import jax.numpy as jnp
from jax import lax
from jax.experimental import pallas as pl
from jax.experimental.pallas import tpu as pltpu
from jax.sharding import PartitionSpec as P

HEAD_DIM = 128
EPS = 1e-06
MESH = pl.DeviceIdType.MESH
F32 = jnp.float32
BF16 = jnp.bfloat16
CHUNKS = 4
GROUP = 4


def dot_nn(a, b):
    return lax.dot_general(a, b, (((1,), (0,)), ((), ())), preferred_element_type=F32)


def dot_nt(a, b):
    return lax.dot_general(a, b, (((1,), (1,)), ((), ())), preferred_element_type=F32)


def dot_tn(a, b):
    return lax.dot_general(a, b, (((0,), (0,)), ((), ())), preferred_element_type=F32)


def body(
    n_seq, n_head,
    q_h, k_h, v_h, gate_h, gain_h, go_h,
    gqv, ggv, acc_a, acc_b, suf, k, v,
    q, gate, gain, go,
    wsend, wbuf, g2, attn, d_o, arows,
    st, st_p, st_c, st_o, st_r, pre,
    gst, gst_p, gst_c, gst_o, gst_r,
    scores, squares, crossed, stat_s, stat_r, inv_b, c_b,
    in_sem, part_sem,
    w_ss, w_rs, a_ss, a_rs, s_ss, s_rs,
    m_ss, m_rs, c_ss, c_rs, r_ss, r_rs,
    gm_ss, gm_rs, gc_ss, gc_rs, gr_ss, gr_rs,
):
    hd = HEAD_DIM
    tok, cols = q.shape
    rows, width = gate.shape
    heads = cols // hd
    half = tok // 2
    mine = heads // 2
    n_pair = mine // 2
    chunk = cols // CHUNKS
    idx = lax.axis_index("seq")
    me = lax.axis_index("head")
    side = lax.rem(idx, 2)
    partner = idx + 1 - 2 * side
    has_below = idx >= 2
    has_above = idx + 2 < n_seq
    n_x = n_head // 2
    at_x = me // 2
    core = lax.rem(me, 2)
    peers = [(dx, dc) for dx in range(1, n_x) for dc in range(2)] + [(0, 1)]
    crossing = list(range(len(peers) - 1))
    beside = len(peers) - 1
    own_head = side * mine
    mate_head = (1 - side) * mine

    def to_peer(p):
        dx, dc = peers[p]
        return lax.rem(at_x + dx, n_x) * 2 + lax.rem(core + dc, 2)

    def from_peer(p):
        dx, dc = peers[p]
        return lax.rem(at_x + n_x - dx, n_x) * 2 + lax.rem(core + dc, 2)

    def row_block(shard):
        return pl.ds(pl.multiple_of(shard * rows, rows), rows)

    def col_block(shard):
        return pl.ds(pl.multiple_of(shard * cols, cols), cols)

    def col_chunk(shard, c):
        return pl.ds(pl.multiple_of(shard * cols + c * chunk, chunk), chunk)

    def head_cols(h):
        return pl.ds(pl.multiple_of(h * hd, hd), hd)

    whole_loads = [
        pltpu.make_async_copy(src, dst, in_sem.at[i])
        for i, (src, dst) in enumerate(((gain_h, gain), (k_h, k), (v_h, v), (q_h, q)))
    ]

    def part_load(i, shard):
        at = col_block(shard)
        return [
            pltpu.make_async_copy(gate_h.at[:, at], gate.at[:, at], part_sem.at[2 * i]),
            pltpu.make_async_copy(go_h.at[:, at], go.at[:, at], part_sem.at[2 * i + 1]),
        ]

    shards = [to_peer(p) for p in range(len(peers))] + [me]
    part_loads = [part_load(i, shard) for i, shard in enumerate(shards)]
    whole_loads[0].start()
    for load in part_loads[0]:
        load.start()
    whole_loads[1].start()
    whole_loads[2].start()
    for part in part_loads[1:]:
        for load in part:
            load.start()
    whole_loads[3].start()

    barrier = pltpu.get_barrier_semaphore()
    for p in range(len(peers)):
        pl.semaphore_signal(barrier, inc=1, device_id={"head": to_peer(p)}, device_id_type=MESH)
    pl.semaphore_signal(barrier, inc=1, device_id={"seq": partner}, device_id_type=MESH)

    @pl.when(has_below)
    def _():
        pl.semaphore_signal(barrier, inc=1, device_id={"seq": idx - 2}, device_id_type=MESH)

    @pl.when(has_above)
    def _():
        pl.semaphore_signal(barrier, inc=1, device_id={"seq": idx + 2}, device_id_type=MESH)

    bc = 256

    def weigh(shard, local):
        def step(i, carry):
            c = pl.multiple_of(i * bc, bc)
            at = pl.ds(pl.multiple_of(shard * cols + c, bc), bc)
            g = gate[:, at].astype(F32)
            scaled = go[:, at].astype(F32) * gain[:, at]
            sig = jax.nn.sigmoid(g)
            part = scaled * sig
            g2[:, at] = part * (1.0 + g * (1.0 - sig))
            weighted = (part * g).astype(BF16)
            if local:
                wbuf[row_block(me), pl.ds(c, bc)] = weighted
            else:
                wsend[:, at] = weighted
            return carry

        lax.fori_loop(0, cols // bc, step, 0)

    def w_copy(p, c):
        to, i = to_peer(p), p * CHUNKS + c
        return pltpu.make_async_remote_copy(
            src_ref=wsend.at[:, col_chunk(to, c)],
            dst_ref=wbuf.at[row_block(me), col_chunk(0, c)],
            send_sem=w_ss.at[i], recv_sem=w_rs.at[i],
            device_id={"head": to}, device_id_type=MESH,
        )

    def w_arrival(p, c):
        to, i = to_peer(p), p * CHUNKS + c
        return pltpu.make_async_remote_copy(
            src_ref=wsend.at[:, col_chunk(to, c)],
            dst_ref=wbuf.at[row_block(from_peer(p)), col_chunk(0, c)],
            send_sem=w_ss.at[i], recv_sem=w_rs.at[i],
            device_id={"head": to}, device_id_type=MESH,
        )

    def a_copy(p, c):
        to, i = to_peer(p), p * CHUNKS + c
        return pltpu.make_async_remote_copy(
            src_ref=attn.at[row_block(to), col_chunk(0, c)],
            dst_ref=arows.at[:, col_chunk(me, c)],
            send_sem=a_ss.at[i], recv_sem=a_rs.at[i],
            device_id={"head": to}, device_id_type=MESH,
        )

    def a_arrival(p, c):
        to, i = to_peer(p), p * CHUNKS + c
        return pltpu.make_async_remote_copy(
            src_ref=attn.at[row_block(to), col_chunk(0, c)],
            dst_ref=arows.at[:, col_chunk(from_peer(p), c)],
            send_sem=a_ss.at[i], recv_sem=a_rs.at[i],
            device_id={"head": to}, device_id_type=MESH,
        )

    def s_copy(p):
        return pltpu.make_async_remote_copy(
            src_ref=stat_s, dst_ref=stat_r.at[p],
            send_sem=s_ss.at[p], recv_sem=s_rs.at[p],
            device_id={"head": to_peer(p)}, device_id_type=MESH,
        )

    def pair_copy(src, dst, ss, rs, base, j, target):
        at = pl.ds(base + 2 * j, 2)
        return pltpu.make_async_remote_copy(
            src_ref=src.at[at], dst_ref=dst.at[at],
            send_sem=ss.at[j], recv_sem=rs.at[j],
            device_id={"seq": target}, device_id_type=MESH,
        )

    def weigh_and_send(p):
        weigh(to_peer(p), False)
        if p == 0:
            below, above = has_below.astype(jnp.int32), has_above.astype(jnp.int32)
            pl.semaphore_wait(barrier, n_head + below + above)
        for c in range(CHUNKS):
            w_copy(p, c).start()

    def wait_part(i):
        for load in part_loads[i]:
            load.wait()

    whole_loads[0].wait()
    wait_part(0)
    weigh_and_send(0)
    whole_loads[1].wait()
    whole_loads[2].wait()

    def states(base, send):
        def step(i, carry):
            first = base + GROUP * i
            for t in range(GROUP):
                sl = head_cols(first + t)
                st[first + t] = dot_tn(k[:, sl], v[:, sl]).astype(BF16)
            if send:
                for t in range(GROUP // 2):
                    pair_copy(st, st_p, m_ss, m_rs, base, i * (GROUP // 2) + t, partner).start()
            return carry

        lax.fori_loop(0, mine // GROUP, step, 0)

    states(mate_head, True)
    for p in range(1, len(peers)):
        wait_part(p)
        weigh_and_send(p)
    states(own_head, False)
    wait_part(len(peers))
    weigh(me, True)
    whole_loads[3].wait()

    def pass_on(j, own, mate, chain, out, given, kept, sems, source_ok, target_ok, target, wants):
        mate_ss, mate_rs, chain_ss, chain_rs, give_ss, give_rs = sems
        at = pl.ds(own_head + 2 * j, 2)
        pair_copy(own, mate, mate_ss, mate_rs, own_head, j, partner).wait_recv()

        @pl.when(source_ok)
        def _():
            pair_copy(out, chain, chain_ss, chain_rs, own_head, j, target).wait_recv()

        @pl.when(jnp.logical_not(source_ok))
        def _():
            chain[at] = jnp.zeros((2, hd, hd), BF16)

        @pl.when(target_ok)
        def _():
            out[at] = (
                chain[at].astype(F32) + mate[at].astype(F32) + own[at].astype(F32)
            ).astype(BF16)
            pair_copy(out, chain, chain_ss, chain_rs, own_head, j, target).start()

        before = chain[at].astype(F32)
        weight = wants.astype(F32)
        given[at] = (before + (1.0 - weight) * own[at].astype(F32)).astype(BF16)
        pair_copy(given, kept, give_ss, give_rs, own_head, j, partner).start()
        kept[at] = (before + weight * mate[at].astype(F32)).astype(BF16)

    at_row = lax.broadcasted_iota(jnp.int32, (half, half), 0)
    at_col = lax.broadcasted_iota(jnp.int32, (half, half), 1)

    def lower(x):
        return jnp.where(at_row >= at_col, x, 0.0).astype(BF16)

    def upper(x):
        return jnp.where(at_row <= at_col, x, 0.0).astype(BF16)

    depth = idx // 2
    length = n_seq // 2

    def forward_local(h):
        sl = head_cols(h)
        q0, q1 = q[:half, sl], q[half:, sl]
        k0, k1 = k[:half, sl], k[half:, sl]
        v0, v1 = v[:half, sl], v[half:, sl]
        acc_a[:half, sl] = dot_nn(lower(dot_nt(q0, k0)), v0)
        acc_a[half:, sl] = dot_nn(dot_nt(q1, k0).astype(BF16), v0) + dot_nn(
            lower(dot_nt(q1, k1)), v1
        )
        scores[h, 0] = upper(dot_nt(k0, q0))
        scores[h, 1] = dot_nt(k0, q1).astype(BF16)
        scores[h, 2] = upper(dot_nt(k1, q1))

    def attend(first):
        for t in range(2):
            sl = head_cols(first + t)
            attn[:, sl] = (acc_a[:, sl] + dot_nn(q[:, sl], pre[first + t])).astype(BF16)

    late = jnp.maximum(depth + 2, n_pair)

    def forward(i, carry):
        @pl.when(i < 2 * n_pair)
        def _():
            for t in range(2):
                forward_local(lax.rem(own_head + 2 * i + t, heads))

        j = i - depth

        @pl.when((j >= 0) & (j < n_pair))
        def _():
            pass_on(
                j, st, st_p, st_c, st_o, st_r, pre,
                (m_ss, m_rs, c_ss, c_rs, r_ss, r_rs),
                has_below, has_above, idx + 2, side,
            )
            attend(own_head + 2 * j)

        m = i - late

        @pl.when((m >= 0) & (m < n_pair))
        def _():
            pair_copy(st_r, pre, r_ss, r_rs, mate_head, m, partner).wait_recv()
            attend(mate_head + 2 * m)

        return carry

    lax.fori_loop(0, max(length + 1 + n_pair, 2 * n_pair), forward, 0)

    br = 128

    def sums(c, carry):
        for p in range(len(peers)):
            w_arrival(p, c).wait_recv()

        def step(i, inner):
            rs = pl.ds(pl.multiple_of(i * br, br), br)
            s0 = jnp.zeros((br, hd), F32)
            s1 = jnp.zeros((br, hd), F32)
            for u in range(chunk // hd):
                at = pl.ds(pl.multiple_of(c * chunk + u * hd, hd), hd)
                a = attn[rs, at].astype(F32)
                w = wbuf[rs, at].astype(F32)
                s0 = s0 + a * a
                s1 = s1 + a * w
            squares[rs, :] += s0
            crossed[rs, :] += s1
            return inner

        lax.fori_loop(0, tok // br, step, 0)
        return carry

    squares[...] = jnp.zeros_like(squares)
    crossed[...] = jnp.zeros_like(crossed)
    lax.fori_loop(0, CHUNKS, sums, 0)
    n_row = tok // hd
    s0 = jnp.sum(jnp.transpose(squares[...]), axis=0, keepdims=True)
    s1 = jnp.sum(jnp.transpose(crossed[...]), axis=0, keepdims=True)
    for r in range(n_row):
        stat_s[r:r + 1, :] = s0[:, r * hd:(r + 1) * hd]
        stat_s[n_row + r:n_row + r + 1, :] = s1[:, r * hd:(r + 1) * hd]
    for p in range(len(peers)):
        s_copy(p).start()
    for c in range(CHUNKS):
        for p in range(len(peers)):
            a_copy(p, c).start()
    total = stat_s[...]
    for p in range(len(peers)):
        s_copy(p).wait_recv()
    for p in range(len(peers)):
        total = total + stat_r[p]
    inv = lax.rsqrt(total[:n_row] / width + EPS)
    c_all = inv * inv * (total[n_row:2 * n_row] / width)
    for r in range(n_row):
        inv_b[r * hd:(r + 1) * hd, :] = jnp.transpose(
            jnp.broadcast_to(inv[r:r + 1], (hd, hd))
        )
        c_b[r * hd:(r + 1) * hd, :] = jnp.transpose(
            jnp.broadcast_to(c_all[r:r + 1], (hd, hd))
        )

    def grads(base, send):
        def step(i, carry):
            first = base + GROUP * i
            for t in range(GROUP):
                sl = head_cols(first + t)
                a = attn[:, sl].astype(F32)
                grad = (inv_b[...] * (wbuf[:, sl].astype(F32) - a * c_b[...])).astype(BF16)
                d_o[:, sl] = grad
                gst[first + t] = dot_tn(q[:, sl], grad).astype(BF16)
            if send:
                for t in range(GROUP // 2):
                    pair_copy(gst, gst_p, gm_ss, gm_rs, base, i * (GROUP // 2) + t, partner).start()
            return carry

        lax.fori_loop(0, mine // GROUP, step, 0)

    grads(mate_head, True)
    grads(own_head, False)

    def backward_local(h):
        sl = head_cols(h)
        q0, q1 = q[:half, sl], q[half:, sl]
        k0, k1 = k[:half, sl], k[half:, sl]
        v0, v1 = v[:half, sl], v[half:, sl]
        d0, d1 = d_o[:half, sl], d_o[half:, sl]
        before = pre[h]
        gqv[:half, sl] = (dot_nn(lower(dot_nt(d0, v0)), k0) + dot_nt(d0, before)).astype(BF16)
        gqv[half:, sl] = (
            dot_nn(dot_nt(d1, v0).astype(BF16), k0)
            + dot_nn(lower(dot_nt(d1, v1)), k1)
            + dot_nt(d1, before)
        ).astype(BF16)
        acc_a[:half, sl] = dot_nn(upper(dot_nt(v0, d0)), q0) + dot_nn(
            dot_nt(v0, d1).astype(BF16), q1
        )
        acc_a[half:, sl] = dot_nn(upper(dot_nt(v1, d1)), q1)
        acc_b[:half, sl] = dot_nn(scores[h, 0], d0) + dot_nn(scores[h, 1], d1)
        acc_b[half:, sl] = dot_nn(scores[h, 2], d1)

    above_me = length - 1 - depth
    back_lag = (3 * above_me + 1) // 2

    def backward(i, carry):
        @pl.when(i < 2 * n_pair)
        def _():
            for t in range(2):
                backward_local(2 * i + t)

        j = i - back_lag

        @pl.when((j >= 0) & (j < n_pair))
        def _():
            pass_on(
                j, gst, gst_p, gst_c, gst_o, gst_r, suf,
                (gm_ss, gm_rs, gc_ss, gc_rs, gr_ss, gr_rs),
                has_above, has_below, idx - 2, 1 - side,
            )

        return carry

    lax.fori_loop(0, max(2 * n_pair, (3 * (length - 1) + 1) // 2 + n_pair), backward, 0)

    def finish(shard, c, local):
        scale = inv_b[row_block(me), :]
        for u in range(chunk // hd):
            at = pl.ds(pl.multiple_of(shard * cols + c * chunk + u * hd, hd), hd)
            if local:
                here = pl.ds(pl.multiple_of(c * chunk + u * hd, hd), hd)
                a = attn[row_block(me), here]
            else:
                a = arows[:, at]
            ggv[:, at] = (g2[:, at] * (a.astype(F32) * scale)).astype(BF16)

    def finish_local(c, carry):
        finish(me, c, True)
        return carry

    lax.fori_loop(0, CHUNKS, finish_local, 0)

    def finish_beside(c, carry):
        a_arrival(beside, c).wait_recv()
        finish(from_peer(beside), c, False)
        return carry

    lax.fori_loop(0, CHUNKS, finish_beside, 0)

    def drain(j, carry):
        pair_copy(st, st_p, m_ss, m_rs, mate_head, j, partner).wait_send()
        pair_copy(st_r, pre, r_ss, r_rs, own_head, j, partner).wait_send()
        pair_copy(gst, gst_p, gm_ss, gm_rs, mate_head, j, partner).wait_send()
        pair_copy(gst_r, suf, gr_ss, gr_rs, own_head, j, partner).wait_send()
        pair_copy(gst_r, suf, gr_ss, gr_rs, mate_head, j, partner).wait_recv()

        @pl.when(has_above)
        def _():
            pair_copy(st_o, st_c, c_ss, c_rs, own_head, j, idx + 2).wait_send()

        @pl.when(has_below)
        def _():
            pair_copy(gst_o, gst_c, gc_ss, gc_rs, own_head, j, idx - 2).wait_send()

        return carry

    lax.fori_loop(0, n_pair, drain, 0)
    for p in range(len(peers)):
        s_copy(p).wait_send()
        for c in range(CHUNKS):
            w_copy(p, c).wait_send()

    def finish_crossing(c, carry):
        for p in crossing:
            a_arrival(p, c).wait_recv()
            finish(from_peer(p), c, False)
        return carry

    lax.fori_loop(0, CHUNKS, finish_crossing, 0)
    for p in range(len(peers)):
        for c in range(CHUNKS):
            a_copy(p, c).wait_send()


def store(gq, gg, acc_a, acc_b, suf, k, v, gq_h, gk_h, gv_h, gg_h, gk, gv, sem, k_sem, v_sem):
    hd = HEAD_DIM
    tok, cols = gq.shape
    span = GROUP * hd
    ready = [
        pltpu.make_async_copy(src, dst, sem.at[i])
        for i, (src, dst) in enumerate(((gq, gq_h), (gg, gg_h)))
    ]
    for copy in ready:
        copy.start()

    def copies(i):
        at = pl.ds(pl.multiple_of(i * span, span), span)
        return (
            pltpu.make_async_copy(gk.at[:, at], gk_h.at[:, at], k_sem.at[i]),
            pltpu.make_async_copy(gv.at[:, at], gv_h.at[:, at], v_sem.at[i]),
        )

    def add_later(i, carry):
        for t in range(GROUP):
            h = GROUP * i + t
            sl = pl.ds(pl.multiple_of(h * hd, hd), hd)
            after = suf[h]
            gk[:, sl] = (acc_a[:, sl] + dot_nt(v[:, sl], after)).astype(BF16)
            gv[:, sl] = (acc_b[:, sl] + dot_nn(k[:, sl], after)).astype(BF16)
        for copy in copies(i):
            copy.start()
        return carry

    groups = cols // span
    lax.fori_loop(0, groups, add_later, 0)
    for copy in ready:
        copy.wait()
    for i in range(groups):
        for copy in copies(i):
            copy.wait()


def on_device(n_seq, n_head, query, key_in, value, gate, gain, grad_out):
    tok, cols = query.shape
    rows, width = gate.shape
    heads = cols // HEAD_DIM
    groups = heads // GROUP
    wide = pltpu.VMEM((tok, cols), BF16)
    thin = pltpu.VMEM((rows, width), BF16)
    state = pltpu.VMEM((heads, HEAD_DIM, HEAD_DIM), BF16)
    token = pltpu.VMEM((tok, HEAD_DIM), F32)
    sum_of = pltpu.VMEM((tok, cols), F32)
    tile = (2 * tok // HEAD_DIM, HEAD_DIM)
    by_part = pltpu.SemaphoreType.DMA(((n_head - 1) * CHUNKS,))
    by_peer = pltpu.SemaphoreType.DMA((n_head - 1,))
    by_pair = pltpu.SemaphoreType.DMA((heads // 4,))
    anywhere = pl.BlockSpec(memory_space=pl.ANY)
    on_chip = pl.BlockSpec(memory_space=pltpu.VMEM)
    results = pl.pallas_call(
        functools.partial(body, n_seq, n_head),
        out_shape=[wide, thin, sum_of, sum_of, state, wide, wide],
        in_specs=[anywhere] * 6,
        out_specs=[on_chip] * 7,
        scratch_shapes=[
            wide, thin, pltpu.VMEM((1, width), F32), thin,
            thin, wide, pltpu.VMEM((rows, width), F32), wide, wide, thin,
            state, state, state, state, state, state,
            state, state, state, state, state,
            pltpu.VMEM((heads, 3, tok // 2, tok // 2), BF16),
            token, token, pltpu.VMEM(tile, F32), pltpu.VMEM((n_head - 1, *tile), F32), token, token,
            pltpu.SemaphoreType.DMA((4,)), pltpu.SemaphoreType.DMA((2 * n_head,)),
            by_part, by_part, by_part, by_part, by_peer, by_peer,
            by_pair, by_pair, by_pair, by_pair, by_pair, by_pair,
            by_pair, by_pair, by_pair, by_pair, by_pair, by_pair,
        ],
        compiler_params=pltpu.CompilerParams(
            collective_id=0, has_side_effects=True, vmem_limit_bytes=44 * 2**20
        ),
        name="linear_attention_backward",
    )(query, key_in, value, gate, gain.reshape(1, width), grad_out)
    wide_out = jax.ShapeDtypeStruct((tok, cols), BF16)
    return pl.pallas_call(
        store,
        out_shape=[wide_out, wide_out, wide_out, jax.ShapeDtypeStruct((rows, width), BF16)],
        in_specs=[on_chip] * 7,
        out_specs=[anywhere] * 4,
        scratch_shapes=[
            wide, wide, pltpu.SemaphoreType.DMA((2,)),
            pltpu.SemaphoreType.DMA((groups,)), pltpu.SemaphoreType.DMA((groups,)),
        ],
        compiler_params=pltpu.CompilerParams(vmem_limit_bytes=6 * 2**20),
        name="store_gradients",
    )(*[pltpu.with_memory_space_constraint(x, pltpu.VMEM) for x in results])


def solution(mesh):
    in_specs = (
        P("seq", "head"),
        P("seq", "head"),
        P("seq", "head"),
        P(("seq", "head"), None),
        P(),
        P(("seq", "head"), None),
    )
    out_specs = (P("seq", "head"), P("seq", "head"), P("seq", "head"), P(("seq", "head"), None))
    return jax.shard_map(
        functools.partial(on_device, mesh.shape["seq"], mesh.shape["head"]),
        mesh=mesh, in_specs=in_specs, out_specs=out_specs, check_vma=False,
    )
```

time: 79.2 us -> 64.5 us (0.81)
  Pallas kernels: 78.4 us -> 63.7 us
    pallas_call x2, Pallas kernels: 78.4 us -> 63.7 us  [the longest x1 60.3 us: on_device(): pl.pallas_call(functools.partial(body, n_seq, n_head), out_shape=[wide, t...]
where the time goes in v1:
time: 64.5 us; the launch traced here: 64.4 us
  Pallas kernels  63.7 us (99%)
    pallas_call x1, Pallas kernels, on_device(): pl.pallas_call(functools.partial(body, n_seq, n_head), out_shape=[wide, t...  60.3 us
    pallas_call x1, Pallas kernels, on_device(): pl.pallas_call(store, out_shape=[wide_out, wide_out, wide_out, jax.ShapeD...  3.45 us

profile of v1, /device:TPU:0, one launch (start us, length us, event | category | flops | bytes accessed | tf_op | source)
XLA Modules:
  0.0 64.4 jit_solution(11661825094292794766)
XLA Ops:
  0.6 60.3 %linear_attention_backward.1 = (bf16[512,2048]{1,0:T(8,128)(2,1)S(1)}, bf16[128,8192]{1,0:T(8,128)(2,1)S(1)}, f32[512,2048]{1,0:T(8,128)S(1)}, f32[512,2048]{1,0...) custom-call(bf16[512,2048]{1,0:T(8,128)(2,1)} %q_h.1, ...), custom_call_target="tpu_custom_call" | custom-call | tf_op jit(solution)/shard_map/linear_attention_backward/pallas_call | solution.py:549
  60.9 3.4 %store_gradients.1 = (bf16[512,2048]{1,0:T(8,128)(2,1)}, bf16[512,2048]{1,0:T(8,128)(2,1)}, bf16[512,2048]{1,0:T(8,128)(2,1)}, bf16[128,8192]{1,0:T(8,128)(2,1)}) custom-call(bf16[512,2048]{1,0:T(8,128)(2,1)S(1)} %get-tuple-element.11.gq, bf16[128,8192]{1,0:T(8,128)(2,1)S(1)} %get-tuple-element.12.gg, f32[512,2048]{1,0:T(8,128)S(1)} %get-tuple-element.13.acc_a, ...), custom_call_target="tpu_custom_call" | custom-call | tf_op jit(solution)/shard_map/store_gradients/pallas_call | solution.py:572

commit v2 on v1

--- a/solution.py
+++ b/solution.py
@@ -14,6 +14,9 @@
 BF16 = jnp.bfloat16
 CHUNKS = 4
 GROUP = 4
+FORWARD_LAG = 3
+BACKWARD_LAG = 3
+GIVE_LAG = 3
 
 
 def dot_nn(a, b):
@@ -36,11 +39,11 @@
     wsend, wbuf, g2, attn, d_o, arows,
     st, st_p, st_c, st_o, st_r, pre,
     gst, gst_p, gst_c, gst_o, gst_r,
-    scores, squares, crossed, stat_s, stat_r, inv_b, c_b,
-    in_sem, part_sem,
+    scores, low_a, up_a, low_b, up_b, squares, crossed, stat_s, stat_r, inv_b, c_b,
+    in_sem, part_sem, first_sem,
     w_ss, w_rs, a_ss, a_rs, s_ss, s_rs,
     m_ss, m_rs, c_ss, c_rs, r_ss, r_rs,
-    gm_ss, gm_rs, gc_ss, gc_rs, gr_ss, gr_rs,
+    gm_ss, gc_ss, gr_ss,
 ):
     hd = HEAD_DIM
     tok, cols = q.shape
@@ -48,7 +51,6 @@
     heads = cols // hd
     half = tok // 2
     mine = heads // 2
-    n_pair = mine // 2
     chunk = cols // CHUNKS
     idx = lax.axis_index("seq")
     me = lax.axis_index("head")
@@ -99,9 +101,18 @@
 
     shards = [to_peer(p) for p in range(len(peers))] + [me]
     part_loads = [part_load(i, shard) for i, shard in enumerate(shards)]
+
+    def first_load(c):
+        at = col_chunk(shards[0], c)
+        return [
+            pltpu.make_async_copy(gate_h.at[:, at], gate.at[:, at], first_sem.at[2 * c]),
+            pltpu.make_async_copy(go_h.at[:, at], go.at[:, at], first_sem.at[2 * c + 1]),
+        ]
+
     whole_loads[0].start()
-    for load in part_loads[0]:
-        load.start()
+    for c in range(CHUNKS):
+        for load in first_load(c):
+            load.start()
     whole_loads[1].start()
     whole_loads[2].start()
     for part in part_loads[1:]:
@@ -122,11 +133,11 @@
     def _():
         pl.semaphore_signal(barrier, inc=1, device_id={"seq": idx + 2}, device_id_type=MESH)
 
-    bc = 256
-
-    def weigh(shard, local):
+    bc = min(256, chunk)
+
+    def weigh(shard, first, span, local):
         def step(i, carry):
-            c = pl.multiple_of(i * bc, bc)
+            c = pl.multiple_of(first + i * bc, bc)
             at = pl.ds(pl.multiple_of(shard * cols + c, bc), bc)
             g = gate[:, at].astype(F32)
             scaled = go[:, at].astype(F32) * gain[:, at]
@@ -140,14 +151,14 @@
                 wsend[:, at] = weighted
             return carry
 
-        lax.fori_loop(0, cols // bc, step, 0)
+        lax.fori_loop(0, span // bc, step, 0)
 
     def w_copy(p, c):
         to, i = to_peer(p), p * CHUNKS + c
         return pltpu.make_async_remote_copy(
             src_ref=wsend.at[:, col_chunk(to, c)],
             dst_ref=wbuf.at[row_block(me), col_chunk(0, c)],
-            send_sem=w_ss.at[i], recv_sem=w_rs.at[i],
+            send_sem=w_ss, recv_sem=w_rs.at[i],
             device_id={"head": to}, device_id_type=MESH,
         )
 
@@ -156,7 +167,7 @@
         return pltpu.make_async_remote_copy(
             src_ref=wsend.at[:, col_chunk(to, c)],
             dst_ref=wbuf.at[row_block(from_peer(p)), col_chunk(0, c)],
-            send_sem=w_ss.at[i], recv_sem=w_rs.at[i],
+            send_sem=w_ss, recv_sem=w_rs.at[i],
             device_id={"head": to}, device_id_type=MESH,
         )
 
@@ -165,7 +176,7 @@
         return pltpu.make_async_remote_copy(
             src_ref=attn.at[row_block(to), col_chunk(0, c)],
             dst_ref=arows.at[:, col_chunk(me, c)],
-            send_sem=a_ss.at[i], recv_sem=a_rs.at[i],
+            send_sem=a_ss, recv_sem=a_rs.at[i],
             device_id={"head": to}, device_id_type=MESH,
         )
 
@@ -174,7 +185,7 @@
         return pltpu.make_async_remote_copy(
             src_ref=attn.at[row_block(to), col_chunk(0, c)],
             dst_ref=arows.at[:, col_chunk(from_peer(p), c)],
-            send_sem=a_ss.at[i], recv_sem=a_rs.at[i],
+            send_sem=a_ss, recv_sem=a_rs.at[i],
             device_id={"head": to}, device_id_type=MESH,
         )
 
@@ -185,19 +196,23 @@
             device_id={"head": to_peer(p)}, device_id_type=MESH,
         )
 
-    def pair_copy(src, dst, ss, rs, base, j, target):
-        at = pl.ds(base + 2 * j, 2)
+    def head_copy(src, dst, ss, rs, base, j, target):
         return pltpu.make_async_remote_copy(
+            src_ref=src.at[base + j], dst_ref=dst.at[base + j],
+            send_sem=ss, recv_sem=rs.at[j],
+            device_id={"seq": target}, device_id_type=MESH,
+        )
+
+    def heads_sent(src, dst, ss, rs, base, target):
+        at = pl.ds(base, mine)
+        pltpu.make_async_remote_copy(
             src_ref=src.at[at], dst_ref=dst.at[at],
-            send_sem=ss.at[j], recv_sem=rs.at[j],
+            send_sem=ss, recv_sem=rs.at[0],
             device_id={"seq": target}, device_id_type=MESH,
-        )
+        ).wait_send()
 
     def weigh_and_send(p):
-        weigh(to_peer(p), False)
-        if p == 0:
-            below, above = has_below.astype(jnp.int32), has_above.astype(jnp.int32)
-            pl.semaphore_wait(barrier, n_head + below + above)
+        weigh(to_peer(p), 0, cols, False)
         for c in range(CHUNKS):
             w_copy(p, c).start()
 
@@ -206,8 +221,14 @@
             load.wait()
 
     whole_loads[0].wait()
-    wait_part(0)
-    weigh_and_send(0)
+    for c in range(CHUNKS):
+        for load in first_load(c):
+            load.wait()
+        weigh(shards[0], c * chunk, chunk, False)
+        if c == 0:
+            below, above = has_below.astype(jnp.int32), has_above.astype(jnp.int32)
+            pl.semaphore_wait(barrier, n_head + below + above)
+        w_copy(0, c).start()
     whole_loads[1].wait()
     whole_loads[2].wait()
 
@@ -218,8 +239,8 @@
                 sl = head_cols(first + t)
                 st[first + t] = dot_tn(k[:, sl], v[:, sl]).astype(BF16)
             if send:
-                for t in range(GROUP // 2):
-                    pair_copy(st, st_p, m_ss, m_rs, base, i * (GROUP // 2) + t, partner).start()
+                for t in range(GROUP):
+                    head_copy(st, st_p, m_ss, m_rs, base, i * GROUP + t, partner).start()
             return carry
 
         lax.fori_loop(0, mine // GROUP, step, 0)
@@ -230,33 +251,33 @@
         weigh_and_send(p)
     states(own_head, False)
     wait_part(len(peers))
-    weigh(me, True)
+    weigh(me, 0, cols, True)
     whole_loads[3].wait()
 
     def pass_on(j, own, mate, chain, out, given, kept, sems, source_ok, target_ok, target, wants):
         mate_ss, mate_rs, chain_ss, chain_rs, give_ss, give_rs = sems
-        at = pl.ds(own_head + 2 * j, 2)
-        pair_copy(own, mate, mate_ss, mate_rs, own_head, j, partner).wait_recv()
+        at = own_head + j
+        head_copy(own, mate, mate_ss, mate_rs, own_head, j, partner).wait_recv()
 
         @pl.when(source_ok)
         def _():
-            pair_copy(out, chain, chain_ss, chain_rs, own_head, j, target).wait_recv()
+            head_copy(out, chain, chain_ss, chain_rs, own_head, j, target).wait_recv()
 
         @pl.when(jnp.logical_not(source_ok))
         def _():
-            chain[at] = jnp.zeros((2, hd, hd), BF16)
+            chain[at] = jnp.zeros((hd, hd), BF16)
 
         @pl.when(target_ok)
         def _():
             out[at] = (
                 chain[at].astype(F32) + mate[at].astype(F32) + own[at].astype(F32)
             ).astype(BF16)
-            pair_copy(out, chain, chain_ss, chain_rs, own_head, j, target).start()
+            head_copy(out, chain, chain_ss, chain_rs, own_head, j, target).start()
 
         before = chain[at].astype(F32)
         weight = wants.astype(F32)
         given[at] = (before + (1.0 - weight) * own[at].astype(F32)).astype(BF16)
-        pair_copy(given, kept, give_ss, give_rs, own_head, j, partner).start()
+        head_copy(given, kept, give_ss, give_rs, own_head, j, partner).start()
         kept[at] = (before + weight * mate[at].astype(F32)).astype(BF16)
 
     at_row = lax.broadcasted_iota(jnp.int32, (half, half), 0)
@@ -284,40 +305,42 @@
         scores[h, 1] = dot_nt(k0, q1).astype(BF16)
         scores[h, 2] = upper(dot_nt(k1, q1))
 
-    def attend(first):
-        for t in range(2):
-            sl = head_cols(first + t)
-            attn[:, sl] = (acc_a[:, sl] + dot_nn(q[:, sl], pre[first + t])).astype(BF16)
-
-    late = jnp.maximum(depth + 2, n_pair)
+    def attend(h):
+        sl = head_cols(h)
+        attn[:, sl] = (acc_a[:, sl] + dot_nn(q[:, sl], pre[h])).astype(BF16)
+
+    late = jnp.maximum(FORWARD_LAG * depth + GIVE_LAG, mine)
 
     def forward(i, carry):
-        @pl.when(i < 2 * n_pair)
-        def _():
-            for t in range(2):
-                forward_local(lax.rem(own_head + 2 * i + t, heads))
-
-        j = i - depth
-
-        @pl.when((j >= 0) & (j < n_pair))
+        j = i - FORWARD_LAG * depth
+        ready = (j >= 0) & (j < mine)
+
+        @pl.when(ready)
         def _():
             pass_on(
                 j, st, st_p, st_c, st_o, st_r, pre,
                 (m_ss, m_rs, c_ss, c_rs, r_ss, r_rs),
                 has_below, has_above, idx + 2, side,
             )
-            attend(own_head + 2 * j)
+
+        @pl.when(i < heads)
+        def _():
+            forward_local(lax.rem(own_head + i, heads))
+
+        @pl.when(ready)
+        def _():
+            attend(own_head + j)
 
         m = i - late
 
-        @pl.when((m >= 0) & (m < n_pair))
+        @pl.when((m >= 0) & (m < mine))
         def _():
-            pair_copy(st_r, pre, r_ss, r_rs, mate_head, m, partner).wait_recv()
-            attend(mate_head + 2 * m)
-
-        return carry
-
-    lax.fori_loop(0, max(length + 1 + n_pair, 2 * n_pair), forward, 0)
+            head_copy(st_r, pre, r_ss, r_rs, mate_head, m, partner).wait_recv()
+            attend(mate_head + m)
+
+        return carry
+
+    lax.fori_loop(0, max(FORWARD_LAG * (length - 1) + GIVE_LAG + mine, heads), forward, 0)
 
     br = 128
 
@@ -371,67 +394,78 @@
             jnp.broadcast_to(c_all[r:r + 1], (hd, hd))
         )
 
-    def grads(base, send):
+    def grads(base, group, send):
         def step(i, carry):
-            first = base + GROUP * i
-            for t in range(GROUP):
+            first = base + group * i
+            for t in range(group):
                 sl = head_cols(first + t)
                 a = attn[:, sl].astype(F32)
                 grad = (inv_b[...] * (wbuf[:, sl].astype(F32) - a * c_b[...])).astype(BF16)
                 d_o[:, sl] = grad
                 gst[first + t] = dot_tn(q[:, sl], grad).astype(BF16)
             if send:
-                for t in range(GROUP // 2):
-                    pair_copy(gst, gst_p, gm_ss, gm_rs, base, i * (GROUP // 2) + t, partner).start()
+                for t in range(group):
+                    head_copy(gst, gst_p, gm_ss, m_rs, base, i * group + t, partner).start()
             return carry
 
-        lax.fori_loop(0, mine // GROUP, step, 0)
-
-    grads(mate_head, True)
-    grads(own_head, False)
-
-    def backward_local(h):
+        lax.fori_loop(0, mine // group, step, 0)
+
+    grads(mate_head, 2, True)
+    grads(own_head, GROUP, False)
+
+    def grad_scores(h, low, up):
+        sl = head_cols(h)
+        v0, v1 = v[:half, sl], v[half:, sl]
+        d0, d1 = d_o[:half, sl], d_o[half:, sl]
+        low[0] = lower(dot_nt(d0, v0))
+        low[1] = dot_nt(d1, v0).astype(BF16)
+        low[2] = lower(dot_nt(d1, v1))
+        up[0] = upper(dot_nt(v0, d0))
+        up[1] = dot_nt(v0, d1).astype(BF16)
+        up[2] = upper(dot_nt(v1, d1))
+
+    def grad_products(h, low, up):
         sl = head_cols(h)
         q0, q1 = q[:half, sl], q[half:, sl]
         k0, k1 = k[:half, sl], k[half:, sl]
-        v0, v1 = v[:half, sl], v[half:, sl]
         d0, d1 = d_o[:half, sl], d_o[half:, sl]
         before = pre[h]
-        gqv[:half, sl] = (dot_nn(lower(dot_nt(d0, v0)), k0) + dot_nt(d0, before)).astype(BF16)
+        gqv[:half, sl] = (dot_nn(low[0], k0) + dot_nt(d0, before)).astype(BF16)
         gqv[half:, sl] = (
-            dot_nn(dot_nt(d1, v0).astype(BF16), k0)
-            + dot_nn(lower(dot_nt(d1, v1)), k1)
-            + dot_nt(d1, before)
+            dot_nn(low[1], k0) + dot_nn(low[2], k1) + dot_nt(d1, before)
         ).astype(BF16)
-        acc_a[:half, sl] = dot_nn(upper(dot_nt(v0, d0)), q0) + dot_nn(
-            dot_nt(v0, d1).astype(BF16), q1
-        )
-        acc_a[half:, sl] = dot_nn(upper(dot_nt(v1, d1)), q1)
+        acc_a[:half, sl] = dot_nn(up[0], q0) + dot_nn(up[1], q1)
+        acc_a[half:, sl] = dot_nn(up[2], q1)
         acc_b[:half, sl] = dot_nn(scores[h, 0], d0) + dot_nn(scores[h, 1], d1)
         acc_b[half:, sl] = dot_nn(scores[h, 2], d1)
 
-    above_me = length - 1 - depth
-    back_lag = (3 * above_me + 1) // 2
+    back_lag = BACKWARD_LAG * (length - 1 - depth)
+    slots = ((low_a, up_a), (low_b, up_b))
 
     def backward(i, carry):
-        @pl.when(i < 2 * n_pair)
-        def _():
-            for t in range(2):
-                backward_local(2 * i + t)
-
-        j = i - back_lag
-
-        @pl.when((j >= 0) & (j < n_pair))
-        def _():
-            pass_on(
-                j, gst, gst_p, gst_c, gst_o, gst_r, suf,
-                (gm_ss, gm_rs, gc_ss, gc_rs, gr_ss, gr_rs),
-                has_above, has_below, idx - 2, 1 - side,
-            )
-
-        return carry
-
-    lax.fori_loop(0, max(2 * n_pair, (3 * (length - 1) + 1) // 2 + n_pair), backward, 0)
+        for t in range(2):
+            h = 2 * i + t
+
+            j = h - back_lag
+
+            @pl.when((j >= 0) & (j < mine))
+            def _():
+                pass_on(
+                    j, gst, gst_p, gst_c, gst_o, gst_r, suf,
+                    (gm_ss, m_rs, gc_ss, c_rs, gr_ss, r_rs),
+                    has_above, has_below, idx - 2, 1 - side,
+                )
+
+            @pl.when(h < heads)
+            def _():
+                grad_products(h, *slots[t])
+                grad_scores(jnp.minimum(h + 1, heads - 1), *slots[1 - t])
+
+        return carry
+
+    steps = max(heads, BACKWARD_LAG * (length - 1) + mine)
+    grad_scores(0, *slots[0])
+    lax.fori_loop(0, (steps + 1) // 2, backward, 0)
 
     def finish(shard, c, local):
         scale = inv_b[row_block(me), :]
@@ -457,29 +491,6 @@
 
     lax.fori_loop(0, CHUNKS, finish_beside, 0)
 
-    def drain(j, carry):
-        pair_copy(st, st_p, m_ss, m_rs, mate_head, j, partner).wait_send()
-        pair_copy(st_r, pre, r_ss, r_rs, own_head, j, partner).wait_send()
-        pair_copy(gst, gst_p, gm_ss, gm_rs, mate_head, j, partner).wait_send()
-        pair_copy(gst_r, suf, gr_ss, gr_rs, own_head, j, partner).wait_send()
-        pair_copy(gst_r, suf, gr_ss, gr_rs, mate_head, j, partner).wait_recv()
-
-        @pl.when(has_above)
-        def _():
-            pair_copy(st_o, st_c, c_ss, c_rs, own_head, j, idx + 2).wait_send()
-
-        @pl.when(has_below)
-        def _():
-            pair_copy(gst_o, gst_c, gc_ss, gc_rs, own_head, j, idx - 2).wait_send()
-
-        return carry
-
-    lax.fori_loop(0, n_pair, drain, 0)
-    for p in range(len(peers)):
-        s_copy(p).wait_send()
-        for c in range(CHUNKS):
-            w_copy(p, c).wait_send()
-
     def finish_crossing(c, carry):
         for p in crossing:
             a_arrival(p, c).wait_recv()
@@ -487,9 +498,38 @@
         return carry
 
     lax.fori_loop(0, CHUNKS, finish_crossing, 0)
+
     for p in range(len(peers)):
-        for c in range(CHUNKS):
-            a_copy(p, c).wait_send()
+        s_copy(p).wait_send()
+    sent = len(peers)
+    pltpu.make_async_remote_copy(
+        src_ref=wsend.at[:, :sent * cols], dst_ref=arows.at[:, :sent * cols],
+        send_sem=w_ss, recv_sem=w_rs.at[0],
+        device_id={"head": to_peer(0)}, device_id_type=MESH,
+    ).wait_send()
+    pltpu.make_async_remote_copy(
+        src_ref=attn.at[:sent * rows], dst_ref=wbuf.at[:sent * rows],
+        send_sem=a_ss, recv_sem=a_rs.at[0],
+        device_id={"head": to_peer(0)}, device_id_type=MESH,
+    ).wait_send()
+    heads_sent(st, st_p, m_ss, m_rs, mate_head, partner)
+    heads_sent(st_r, pre, r_ss, r_rs, own_head, partner)
+    heads_sent(gst, gst_p, gm_ss, m_rs, mate_head, partner)
+
+    @pl.when(has_above)
+    def _():
+        heads_sent(st_o, st_c, c_ss, c_rs, own_head, idx + 2)
+
+    @pl.when(has_below)
+    def _():
+        heads_sent(gst_o, gst_c, gc_ss, c_rs, own_head, idx - 2)
+
+    def given(j, carry):
+        head_copy(gst_r, suf, gr_ss, r_rs, mate_head, j, partner).wait_recv()
+        return carry
+
+    lax.fori_loop(0, mine, given, 0)
+    heads_sent(gst_r, suf, gr_ss, r_rs, own_head, partner)
 
 
 def store(gq, gg, acc_a, acc_b, suf, k, v, gq_h, gk_h, gv_h, gg_h, gk, gv, sem, k_sem, v_sem):
@@ -539,11 +579,13 @@
     thin = pltpu.VMEM((rows, width), BF16)
     state = pltpu.VMEM((heads, HEAD_DIM, HEAD_DIM), BF16)
     token = pltpu.VMEM((tok, HEAD_DIM), F32)
+    blocks = pltpu.VMEM((3, tok // 2, tok // 2), BF16)
     sum_of = pltpu.VMEM((tok, cols), F32)
     tile = (2 * tok // HEAD_DIM, HEAD_DIM)
     by_part = pltpu.SemaphoreType.DMA(((n_head - 1) * CHUNKS,))
+    one = pltpu.SemaphoreType.DMA(())
     by_peer = pltpu.SemaphoreType.DMA((n_head - 1,))
-    by_pair = pltpu.SemaphoreType.DMA((heads // 4,))
+    by_head = pltpu.SemaphoreType.DMA((heads // 2,))
     anywhere = pl.BlockSpec(memory_space=pl.ANY)
     on_chip = pl.BlockSpec(memory_space=pltpu.VMEM)
     results = pl.pallas_call(
@@ -557,11 +599,13 @@
             state, state, state, state, state, state,
             state, state, state, state, state,
             pltpu.VMEM((heads, 3, tok // 2, tok // 2), BF16),
+            blocks, blocks, blocks, blocks,
             token, token, pltpu.VMEM(tile, F32), pltpu.VMEM((n_head - 1, *tile), F32), token, token,
             pltpu.SemaphoreType.DMA((4,)), pltpu.SemaphoreType.DMA((2 * n_head,)),
-            by_part, by_part, by_part, by_part, by_peer, by_peer,
-            by_pair, by_pair, by_pair, by_pair, by_pair, by_pair,
-            by_pair, by_pair, by_pair, by_pair, by_pair, by_pair,
+            pltpu.SemaphoreType.DMA((2 * CHUNKS,)),
+            one, by_part, one, by_part, by_peer, by_peer,
+            one, by_head, one, by_head, one, by_head,
+            one, one, one,
         ],
         compiler_params=pltpu.CompilerParams(
             collective_id=0, has_side_effects=True, vmem_limit_bytes=44 * 2**20

time: 64.5 us -> 59 us (0.915)
  Pallas kernels: 63.7 us -> 58.2 us
    pallas_call x1, Pallas kernels: 60.3 us -> 54.7 us  [on_device(): pl.pallas_call(functools.partial(body, n_seq, n_head), out_shape=[wide, t...]
where the time goes in v2:
time: 59 us; the launch traced here: 58.8 us
  Pallas kernels  58.2 us (99%)
  between operations  0.64 us (1%)
    pallas_call x1, Pallas kernels, on_device(): pl.pallas_call(functools.partial(body, n_seq, n_head), out_shape=[wide, t...  54.7 us
    pallas_call x1, Pallas kernels, on_device(): pl.pallas_call(store, out_shape=[wide_out, wide_out, wide_out, jax.ShapeD...  3.45 us

profile of v2, /device:TPU:0, one launch (start us, length us, event | category | flops | bytes accessed | tf_op | source)
XLA Modules:
  0.0 58.8 jit_solution(2404896081203271022)
XLA Ops:
  0.6 54.7 %linear_attention_backward.1 = (bf16[512,2048]{1,0:T(8,128)(2,1)S(1)}, bf16[128,8192]{1,0:T(8,128)(2,1)S(1)}, f32[512,2048]{1,0:T(8,128)S(1)}, f32[512,2048]{1,0...) custom-call(bf16[512,2048]{1,0:T(8,128)(2,1)} %q_h.1, ...), custom_call_target="tpu_custom_call" | custom-call | tf_op jit(solution)/shard_map/linear_attention_backward/pallas_call | solution.py:591
  55.4 3.4 %store_gradients.1 = (bf16[512,2048]{1,0:T(8,128)(2,1)}, bf16[512,2048]{1,0:T(8,128)(2,1)}, bf16[512,2048]{1,0:T(8,128)(2,1)}, bf16[128,8192]{1,0:T(8,128)(2,1)}) custom-call(bf16[512,2048]{1,0:T(8,128)(2,1)S(1)} %get-tuple-element.11.gq, bf16[128,8192]{1,0:T(8,128)(2,1)S(1)} %get-tuple-element.12.gg, f32[512,2048]{1,0:T(8,128)S(1)} %get-tuple-element.13.acc_a, ...), custom_call_target="tpu_custom_call" | custom-call | tf_op jit(solution)/shard_map/store_gradients/pallas_call | solution.py:616

commit v3 on v2

--- a/solution.py
+++ b/solution.py
@@ -15,8 +15,9 @@
 CHUNKS = 4
 GROUP = 4
 FORWARD_LAG = 3
-BACKWARD_LAG = 3
+BACKWARD_LAG = 5
 GIVE_LAG = 3
+PARTS = 1
 
 
 def dot_nn(a, b):
@@ -52,6 +53,7 @@
     half = tok // 2
     mine = heads // 2
     chunk = cols // CHUNKS
+    piece = hd // PARTS
     idx = lax.axis_index("seq")
     me = lax.axis_index("head")
     side = lax.rem(idx, 2)
@@ -62,8 +64,6 @@
     at_x = me // 2
     core = lax.rem(me, 2)
     peers = [(dx, dc) for dx in range(1, n_x) for dc in range(2)] + [(0, 1)]
-    crossing = list(range(len(peers) - 1))
-    beside = len(peers) - 1
     own_head = side * mine
     mate_head = (1 - side) * mine
 
@@ -95,18 +95,17 @@
     def part_load(i, shard):
         at = col_block(shard)
         return [
-            pltpu.make_async_copy(gate_h.at[:, at], gate.at[:, at], part_sem.at[2 * i]),
-            pltpu.make_async_copy(go_h.at[:, at], go.at[:, at], part_sem.at[2 * i + 1]),
+            pltpu.make_async_copy(gate_h.at[:, at], gate.at[:, at], part_sem.at[i]),
+            pltpu.make_async_copy(go_h.at[:, at], go.at[:, at], part_sem.at[i]),
         ]
 
     shards = [to_peer(p) for p in range(len(peers))] + [me]
-    part_loads = [part_load(i, shard) for i, shard in enumerate(shards)]
 
     def first_load(c):
         at = col_chunk(shards[0], c)
         return [
-            pltpu.make_async_copy(gate_h.at[:, at], gate.at[:, at], first_sem.at[2 * c]),
-            pltpu.make_async_copy(go_h.at[:, at], go.at[:, at], first_sem.at[2 * c + 1]),
+            pltpu.make_async_copy(gate_h.at[:, at], gate.at[:, at], first_sem.at[c]),
+            pltpu.make_async_copy(go_h.at[:, at], go.at[:, at], first_sem.at[c]),
         ]
 
     whole_loads[0].start()
@@ -115,8 +114,8 @@
             load.start()
     whole_loads[1].start()
     whole_loads[2].start()
-    for part in part_loads[1:]:
-        for load in part:
+    for i in range(1, len(shards)):
+        for load in part_load(i, shards[i]):
             load.start()
     whole_loads[3].start()
 
@@ -154,52 +153,58 @@
         lax.fori_loop(0, span // bc, step, 0)
 
     def w_copy(p, c):
-        to, i = to_peer(p), p * CHUNKS + c
+        to = to_peer(p)
         return pltpu.make_async_remote_copy(
             src_ref=wsend.at[:, col_chunk(to, c)],
             dst_ref=wbuf.at[row_block(me), col_chunk(0, c)],
-            send_sem=w_ss, recv_sem=w_rs.at[i],
+            send_sem=w_ss, recv_sem=w_rs.at[c],
             device_id={"head": to}, device_id_type=MESH,
         )
 
-    def w_arrival(p, c):
-        to, i = to_peer(p), p * CHUNKS + c
-        return pltpu.make_async_remote_copy(
-            src_ref=wsend.at[:, col_chunk(to, c)],
-            dst_ref=wbuf.at[row_block(from_peer(p)), col_chunk(0, c)],
-            send_sem=w_ss, recv_sem=w_rs.at[i],
-            device_id={"head": to}, device_id_type=MESH,
-        )
+    def w_arrivals(c):
+        sent = len(peers) * rows
+        pltpu.make_async_remote_copy(
+            src_ref=attn.at[:sent, col_chunk(0, c)], dst_ref=wbuf.at[:sent, col_chunk(0, c)],
+            send_sem=w_ss, recv_sem=w_rs.at[c],
+            device_id={"head": to_peer(0)}, device_id_type=MESH,
+        ).wait_recv()
 
     def a_copy(p, c):
-        to, i = to_peer(p), p * CHUNKS + c
+        to = to_peer(p)
         return pltpu.make_async_remote_copy(
             src_ref=attn.at[row_block(to), col_chunk(0, c)],
             dst_ref=arows.at[:, col_chunk(me, c)],
-            send_sem=a_ss, recv_sem=a_rs.at[i],
+            send_sem=a_ss, recv_sem=a_rs.at[c],
             device_id={"head": to}, device_id_type=MESH,
         )
 
-    def a_arrival(p, c):
-        to, i = to_peer(p), p * CHUNKS + c
-        return pltpu.make_async_remote_copy(
-            src_ref=attn.at[row_block(to), col_chunk(0, c)],
-            dst_ref=arows.at[:, col_chunk(from_peer(p), c)],
-            send_sem=a_ss, recv_sem=a_rs.at[i],
-            device_id={"head": to}, device_id_type=MESH,
-        )
+    def a_arrivals(c):
+        sent = len(peers) * rows
+        pltpu.make_async_remote_copy(
+            src_ref=attn.at[:sent, col_chunk(0, c)], dst_ref=wbuf.at[:sent, col_chunk(0, c)],
+            send_sem=a_ss, recv_sem=a_rs.at[c],
+            device_id={"head": to_peer(0)}, device_id_type=MESH,
+        ).wait_recv()
 
     def s_copy(p):
         return pltpu.make_async_remote_copy(
             src_ref=stat_s, dst_ref=stat_r.at[p],
-            send_sem=s_ss.at[p], recv_sem=s_rs.at[p],
+            send_sem=s_ss, recv_sem=s_rs,
             device_id={"head": to_peer(p)}, device_id_type=MESH,
         )
 
-    def head_copy(src, dst, ss, rs, base, j, target):
+    def stats_moved():
         return pltpu.make_async_remote_copy(
-            src_ref=src.at[base + j], dst_ref=dst.at[base + j],
-            send_sem=ss, recv_sem=rs.at[j],
+            src_ref=stat_r, dst_ref=stat_r,
+            send_sem=s_ss, recv_sem=s_rs,
+            device_id={"head": to_peer(0)}, device_id_type=MESH,
+        )
+
+    def head_copy(src, dst, ss, rs, base, j, u, target):
+        at = pl.ds(u * piece, piece)
+        return pltpu.make_async_remote_copy(
+            src_ref=src.at[base + j, at], dst_ref=dst.at[base + j, at],
+            send_sem=ss, recv_sem=rs.at[PARTS * j + u],
             device_id={"seq": target}, device_id_type=MESH,
         )
 
@@ -217,13 +222,15 @@
             w_copy(p, c).start()
 
     def wait_part(i):
-        for load in part_loads[i]:
-            load.wait()
+        pltpu.make_async_copy(
+            gate_h.at[:, :2 * cols], gate.at[:, :2 * cols], part_sem.at[i]
+        ).wait()
 
     whole_loads[0].wait()
     for c in range(CHUNKS):
-        for load in first_load(c):
-            load.wait()
+        pltpu.make_async_copy(
+            gate_h.at[:, :2 * chunk], gate.at[:, :2 * chunk], first_sem.at[c]
+        ).wait()
         weigh(shards[0], c * chunk, chunk, False)
         if c == 0:
             below, above = has_below.astype(jnp.int32), has_above.astype(jnp.int32)
@@ -240,7 +247,8 @@
                 st[first + t] = dot_tn(k[:, sl], v[:, sl]).astype(BF16)
             if send:
                 for t in range(GROUP):
-                    head_copy(st, st_p, m_ss, m_rs, base, i * GROUP + t, partner).start()
+                    for u in range(PARTS):
+                        head_copy(st, st_p, m_ss, m_rs, base, i * GROUP + t, u, partner).start()
             return carry
 
         lax.fori_loop(0, mine // GROUP, step, 0)
@@ -256,29 +264,30 @@
 
     def pass_on(j, own, mate, chain, out, given, kept, sems, source_ok, target_ok, target, wants):
         mate_ss, mate_rs, chain_ss, chain_rs, give_ss, give_rs = sems
-        at = own_head + j
-        head_copy(own, mate, mate_ss, mate_rs, own_head, j, partner).wait_recv()
-
-        @pl.when(source_ok)
-        def _():
-            head_copy(out, chain, chain_ss, chain_rs, own_head, j, target).wait_recv()
-
-        @pl.when(jnp.logical_not(source_ok))
-        def _():
-            chain[at] = jnp.zeros((hd, hd), BF16)
-
-        @pl.when(target_ok)
-        def _():
-            out[at] = (
-                chain[at].astype(F32) + mate[at].astype(F32) + own[at].astype(F32)
-            ).astype(BF16)
-            head_copy(out, chain, chain_ss, chain_rs, own_head, j, target).start()
-
-        before = chain[at].astype(F32)
         weight = wants.astype(F32)
-        given[at] = (before + (1.0 - weight) * own[at].astype(F32)).astype(BF16)
-        head_copy(given, kept, give_ss, give_rs, own_head, j, partner).start()
-        kept[at] = (before + weight * mate[at].astype(F32)).astype(BF16)
+        for u in range(PARTS):
+            at = (own_head + j, slice(u * piece, (u + 1) * piece))
+            head_copy(own, mate, mate_ss, mate_rs, own_head, j, u, partner).wait_recv()
+
+            @pl.when(source_ok)
+            def _():
+                head_copy(out, chain, chain_ss, chain_rs, own_head, j, u, target).wait_recv()
+
+            @pl.when(jnp.logical_not(source_ok))
+            def _():
+                chain[at] = jnp.zeros((piece, hd), BF16)
+
+            @pl.when(target_ok)
+            def _():
+                out[at] = (
+                    chain[at].astype(F32) + mate[at].astype(F32) + own[at].astype(F32)
+                ).astype(BF16)
+                head_copy(out, chain, chain_ss, chain_rs, own_head, j, u, target).start()
+
+            before = chain[at].astype(F32)
+            given[at] = (before + (1.0 - weight) * own[at].astype(F32)).astype(BF16)
+            head_copy(given, kept, give_ss, give_rs, own_head, j, u, partner).start()
+            kept[at] = (before + weight * mate[at].astype(F32)).astype(BF16)
 
     at_row = lax.broadcasted_iota(jnp.int32, (half, half), 0)
     at_col = lax.broadcasted_iota(jnp.int32, (half, half), 1)
@@ -335,7 +344,8 @@
 
         @pl.when((m >= 0) & (m < mine))
         def _():
-            head_copy(st_r, pre, r_ss, r_rs, mate_head, m, partner).wait_recv()
+            for u in range(PARTS):
+                head_copy(st_r, pre, r_ss, r_rs, mate_head, m, u, partner).wait_recv()
             attend(mate_head + m)
 
         return carry
@@ -345,8 +355,7 @@
     br = 128
 
     def sums(c, carry):
-        for p in range(len(peers)):
-            w_arrival(p, c).wait_recv()
+        w_arrivals(c)
 
         def step(i, inner):
             rs = pl.ds(pl.multiple_of(i * br, br), br)
@@ -380,8 +389,7 @@
         for p in range(len(peers)):
             a_copy(p, c).start()
     total = stat_s[...]
-    for p in range(len(peers)):
-        s_copy(p).wait_recv()
+    stats_moved().wait_recv()
     for p in range(len(peers)):
         total = total + stat_r[p]
     inv = lax.rsqrt(total[:n_row] / width + EPS)
@@ -405,7 +413,8 @@
                 gst[first + t] = dot_tn(q[:, sl], grad).astype(BF16)
             if send:
                 for t in range(group):
-                    head_copy(gst, gst_p, gm_ss, m_rs, base, i * group + t, partner).start()
+                    for u in range(PARTS):
+                        head_copy(gst, gst_p, gm_ss, m_rs, base, i * group + t, u, partner).start()
             return carry
 
         lax.fori_loop(0, mine // group, step, 0)
@@ -439,7 +448,8 @@
         acc_b[:half, sl] = dot_nn(scores[h, 0], d0) + dot_nn(scores[h, 1], d1)
         acc_b[half:, sl] = dot_nn(scores[h, 2], d1)
 
-    back_lag = BACKWARD_LAG * (length - 1 - depth)
+    from_end = length - 1 - depth
+    back_lag = BACKWARD_LAG * from_end + jnp.minimum(from_end, 1)
     slots = ((low_a, up_a), (low_b, up_b))
 
     def backward(i, carry):
@@ -463,7 +473,7 @@
 
         return carry
 
-    steps = max(heads, BACKWARD_LAG * (length - 1) + mine)
+    steps = max(heads, BACKWARD_LAG * (length - 1) + 1 + mine)
     grad_scores(0, *slots[0])
     lax.fori_loop(0, (steps + 1) // 2, backward, 0)
 
@@ -484,23 +494,15 @@
 
     lax.fori_loop(0, CHUNKS, finish_local, 0)
 
-    def finish_beside(c, carry):
-        a_arrival(beside, c).wait_recv()
-        finish(from_peer(beside), c, False)
-        return carry
-
-    lax.fori_loop(0, CHUNKS, finish_beside, 0)
-
-    def finish_crossing(c, carry):
-        for p in crossing:
-            a_arrival(p, c).wait_recv()
+    def finish_sent(c, carry):
+        a_arrivals(c)
+        for p in range(len(peers)):
             finish(from_peer(p), c, False)
         return carry
 
-    lax.fori_loop(0, CHUNKS, finish_crossing, 0)
-
-    for p in range(len(peers)):
-        s_copy(p).wait_send()
+    lax.fori_loop(0, CHUNKS, finish_sent, 0)
+
+    stats_moved().wait_send()
     sent = len(peers)
     pltpu.make_async_remote_copy(
         src_ref=wsend.at[:, :sent * cols], dst_ref=arows.at[:, :sent * cols],
@@ -525,7 +527,8 @@
         heads_sent(gst_o, gst_c, gc_ss, c_rs, own_head, idx - 2)
 
     def given(j, carry):
-        head_copy(gst_r, suf, gr_ss, r_rs, mate_head, j, partner).wait_recv()
+        for u in range(PARTS):
+            head_copy(gst_r, suf, gr_ss, r_rs, mate_head, j, u, partner).wait_recv()
         return carry
 
     lax.fori_loop(0, mine, given, 0)
@@ -582,10 +585,9 @@
     blocks = pltpu.VMEM((3, tok // 2, tok // 2), BF16)
     sum_of = pltpu.VMEM((tok, cols), F32)
     tile = (2 * tok // HEAD_DIM, HEAD_DIM)
-    by_part = pltpu.SemaphoreType.DMA(((n_head - 1) * CHUNKS,))
+    by_chunk = pltpu.SemaphoreType.DMA((CHUNKS,))
     one = pltpu.SemaphoreType.DMA(())
-    by_peer = pltpu.SemaphoreType.DMA((n_head - 1,))
-    by_head = pltpu.SemaphoreType.DMA((heads // 2,))
+    by_head = pltpu.SemaphoreType.DMA((heads // 2 * PARTS,))
     anywhere = pl.BlockSpec(memory_space=pl.ANY)
     on_chip = pl.BlockSpec(memory_space=pltpu.VMEM)
     results = pl.pallas_call(
@@ -601,9 +603,8 @@
             pltpu.VMEM((heads, 3, tok // 2, tok // 2), BF16),
             blocks, blocks, blocks, blocks,
             token, token, pltpu.VMEM(tile, F32), pltpu.VMEM((n_head - 1, *tile), F32), token, token,
-            pltpu.SemaphoreType.DMA((4,)), pltpu.SemaphoreType.DMA((2 * n_head,)),
-            pltpu.SemaphoreType.DMA((2 * CHUNKS,)),
-            one, by_part, one, by_part, by_peer, by_peer,
+            pltpu.SemaphoreType.DMA((4,)), pltpu.SemaphoreType.DMA((n_head,)), by_chunk,
+            one, by_chunk, one, by_chunk, one, one,
             one, by_head, one, by_head, one, by_head,
             one, one, one,
         ],

time: 59 us -> 58.6 us (level)
  no operation moved by 1% of the time
where the time goes in v3:
time: 58.6 us; the launch traced here: 58.5 us
  Pallas kernels  57.8 us (99%)
  between operations  0.64 us (1%)
    pallas_call x1, Pallas kernels, on_device(): pl.pallas_call(functools.partial(body, n_seq, n_head), out_shape=[wide, t...  54.4 us
    pallas_call x1, Pallas kernels, on_device(): pl.pallas_call(store, out_shape=[wide_out, wide_out, wide_out, jax.ShapeD...  3.45 us

profile of v3, /device:TPU:0, one launch (start us, length us, event | category | flops | bytes accessed | tf_op | source)
XLA Modules:
  0.0 58.5 jit_solution(12908628228783799201)
XLA Ops:
  0.6 54.4 %linear_attention_backward.1 = (bf16[512,2048]{1,0:T(8,128)(2,1)S(1)}, bf16[128,8192]{1,0:T(8,128)(2,1)S(1)}, f32[512,2048]{1,0:T(8,128)S(1)}, f32[512,2048]{1,0...) custom-call(bf16[512,2048]{1,0:T(8,128)(2,1)} %q_h.1, ...), custom_call_target="tpu_custom_call" | custom-call | tf_op jit(solution)/shard_map/linear_attention_backward/pallas_call | solution.py:593
  55.0 3.5 %store_gradients.1 = (bf16[512,2048]{1,0:T(8,128)(2,1)}, bf16[512,2048]{1,0:T(8,128)(2,1)}, bf16[512,2048]{1,0:T(8,128)(2,1)}, bf16[128,8192]{1,0:T(8,128)(2,1)}) custom-call(bf16[512,2048]{1,0:T(8,128)(2,1)S(1)} %get-tuple-element.11.gq, bf16[128,8192]{1,0:T(8,128)(2,1)S(1)} %get-tuple-element.12.gg, f32[512,2048]{1,0:T(8,128)S(1)} %get-tuple-element.13.acc_a, ...), custom_call_target="tpu_custom_call" | custom-call | tf_op jit(solution)/shard_map/store_gradients/pallas_call | solution.py:617
